TPU v7x, 256 devices: a whole 4x4x8 slice. The times are simulated.
256 devices in a mesh: row: 16 (over x_lo, z), col: 16 (over x_hi, y, core).
Axes of the slice: x: 4 (x_hi: 2, x_lo: 2; x = x_hi * 2 + x_lo), y: 4, z: 8, core: 2. Of those that a mesh axis runs over, the one named last changes fastest.
Arguments:
- tensor: bfloat16 [4096, 2048, 128], P('row', 'col'), may hold values from -96 to 96
- factor_a: float32 [4096, 128], P(('row', 'col')), may hold values from -4.5 to 4.5
- factor_b: float32 [2048, 128], P(('col', 'row')), may hold values from -4.5 to 4.5
- factor_c: float32 [128, 128], replicated, may hold values from -4.5 to 4.5
Outputs:
- new_a: float32 [4096, 128], P(('row', 'col'))
- new_b: float32 [2048, 128], P(('col', 'row'))
- new_c: float32 [128, 128], replicated
All inputs are finite; a program needn't handle non-finite values.
Results may differ from a plain program's by a relative error of at most 0.01.
Values may be sent and summed in bfloat16 or wider, within the bound.
A program may use at most 128 MiB of HBM per device.

v0:
```python
import jax
import jax.numpy as jnp
from jax import lax
from jax.sharding import PartitionSpec as P

STEPS = 2
damping = 0.9
scaling = 0.25
epsilon = 1e-06


def column_squares(values16):
    return jnp.sum(jnp.square(values16.astype(jnp.float32)), axis=0)


def local_terms(block, tile_a, tile_b, c16):
    rows_i, rows_j, depth = block.shape
    rank = tile_a.shape[1]
    pairs = (
        tile_a.astype(jnp.float32)[:, None, :] * tile_b.astype(jnp.float32)[None, :, :]
    ).astype(jnp.bfloat16)
    pairs = pairs.reshape(rows_i * rows_j, rank)
    model = jnp.dot(pairs, c16.T, preferred_element_type=jnp.float32)
    resid = (block.reshape(rows_i * rows_j, depth).astype(jnp.float32) - model).astype(jnp.bfloat16)
    along = jnp.dot(resid, c16, preferred_element_type=jnp.float32).reshape(rows_i, rows_j, rank)
    grad_a = jnp.sum(along * tile_b.astype(jnp.float32)[None, :, :], axis=1)
    grad_b = jnp.sum(along * tile_a.astype(jnp.float32)[:, None, :], axis=0)
    grad_c = lax.dot_general(
        resid, pairs, (((0,), (0,)), ((), ())), preferred_element_type=jnp.float32
    )
    return (grad_a, grad_b, grad_c)


def local(tensor, factor_a, factor_b, factor_c):
    own_a, own_b, third = (factor_a, factor_b, factor_c)
    for step in range(STEPS):
        a_mine16 = own_a.astype(jnp.bfloat16)
        b_mine16 = own_b.astype(jnp.bfloat16)
        tile_a = lax.all_gather(a_mine16, "col", axis=0, tiled=True)
        tile_b = lax.all_gather(b_mine16, "row", axis=0, tiled=True)
        norm_a, norm_b = lax.psum(
            (column_squares(a_mine16), column_squares(b_mine16)), ("row", "col")
        )
        c16 = third.astype(jnp.bfloat16)
        norm_c = column_squares(c16)
        step_a = scaling / (norm_b * norm_c + epsilon)
        step_b = scaling / (norm_a * norm_c + epsilon)
        step_c = scaling / (norm_a * norm_b + epsilon)
        grad_a, grad_b, grad_c = local_terms(tensor, tile_a, tile_b, c16)
        grad_a = lax.psum_scatter(
            grad_a.astype(jnp.bfloat16), "col", scatter_dimension=0, tiled=True
        ).astype(jnp.float32)
        grad_b = lax.psum_scatter(
            grad_b.astype(jnp.bfloat16), "row", scatter_dimension=0, tiled=True
        ).astype(jnp.float32)
        own_a = damping * own_a + step_a * grad_a
        own_b = damping * own_b + step_b * grad_b
        grad_c = lax.psum(grad_c, ("row", "col"))
        third = damping * third + step_c * grad_c
    return (own_a, own_b, third)


def solution(mesh):
    return jax.shard_map(
        local,
        mesh=mesh,
        in_specs=(P("row", "col", None), P(("row", "col"), None), P(("col", "row"), None), P()),
        out_specs=(P(("row", "col"), None), P(("col", "row"), None), P()),
        check_vma=False,
    )
```

profile of v0, /device:TPU:1, one launch (start us, length us, event | category | flops | bytes accessed | tf_op | source)
XLA Modules:
  0.0 663.4 jit_solution(11993279583761159699)
XLA Ops:
  8.1 0.7 multiply_reduce_fusion.9
  8.8 0.7 multiply_reduce_fusion.7
  9.5 30.3 %all_gather.13 = bf16[128,128]{1,0:T(8,128)(2,1)S(1)} all-gather(bf16[8,128]{1,0:T(8,128)(2,1)S(1)} %get-tuple-element.14), channel_id=1, replica_groups=mesh['row'=16,'col'=16] {'row'}, dimensions={0}, use_global_device_ids=true | all-gather | bytes 34816 | tf_op jit(solution)/shard_map/all_gather | solution.py:40
  39.8 31.7 %all_gather.12 = bf16[256,128]{1,0:T(8,128)(2,1)S(1)} all-gather(bf16[16,128]{1,0:T(8,128)(2,1)S(1)} %get-tuple-element.16), channel_id=1, replica_groups=mesh['row'=16,'col'=16] {'col'}, dimensions={0}, use_global_device_ids=true | all-gather | bytes 69632 | tf_op jit(solution)/shard_map/all_gather | solution.py:39
  71.5 5.6 multiply_convert_fusion.1
  77.1 8.1 %fusion.1 = bf16[32768,128]{1,0:T(8,128)(2,1)S(1)} fusion(bf16[32768,128]{1,0:T(8,128)(2,1)} %bitcast.21, bf16[32768,128]{1,0:T(8,128)(2,1)} %bitcast.25, f32[128,128]{1,0:T(8,128)S(1)} %copy-done.2), kind=kOutput, calls=%fused_computation.3 | convolution fusion | flops 1086341120 | bytes 25231360 | tf_op jit(solution)/shard_map/dot_general | solution.py:23
  85.2 3.2 copy-done
  88.5 6.4 fusion.11
  94.9 0.0 reduce-scatter.3.cloned.1.call-start
  94.9 12.1 %multiply_reduce_fusion.3 = (bf16[256,128]{1,0:T(8,128)(2,1)}, f32[32768,128]{1,0:T(8,128)}) fusion(f32[128,128]{1,0:T(8,128)S(1)} %convert_element_type.111, bf16[32768,128]{1,0:T(8,128)(2,1)} %copy-done, f32[128,128]{1,0:T(8,128)S(1)} %copy-done.2), kind=kOutput, calls=%fused_computation.8 | convolution fusion | flops 1082114048 | bytes 25362432 | tf_op jit(solution)/shard_map/dot_general | solution.py:25
  107.1 7.3 %multiply_reduce_fusion.2 = bf16[128,128]{1,0:T(8,128)(2,1)S(1)} fusion(f32[256,128,128]{2,1,0:T(8,128)} %bitcast.23, f32[256,128]{1,0:T(8,128)S(1)} %convert_element_type.110), kind=kLoop, calls=%fused_computation.7 | loop fusion | flops 8372224 | bytes 16941056 | tf_op jit(solution)/shard_map/reduce_sum | solution.py:27
  114.5 46.3 %all-reduce = bf16[128,128]{1,0:T(8,128)(2,1)S(1)} all-reduce(bf16[128,128]{1,0:T(8,128)(2,1)S(1)} %multiply_reduce_fusion.2), channel_id=3, replica_groups=mesh['row'=16,'col'=16] {'row'}, use_global_device_ids=true, to_apply=%region_8.0.clone | all-reduce | flops 16384 | bytes 65536
  160.8 0.6 dynamic-slice
  162.0 84.4 %all-reduce.3 = (f32[128]{0:T(128)S(1)}, f32[128]{0:T(128)S(1)}) all-reduce(f32[128]{0:T(128)S(1)} %get-tuple-element.15, f32[128]{0:T(128)S(1)} %get-tuple-element.13), channel_id=1, replica_groups=mesh['row'=16,'col'=16] {'row','col'}, use_global_device_ids=true, to_apply=%region_6.0 | all-reduce | flops 256 | bytes 2048 | tf_op jit(solution)/shard_map/psum | solution.py:41
  246.4 81.7 %all-reduce.7.cloned.1.call-done = f32[128,128]{1,0:T(8,128)} async-done(((f32[128,128]{1,0:T(8,128)}), f32[128,128]{1,0:T(8,128)}) %all-reduce.7.cloned.1.call-update) | async-done | bytes 65552 | tf_op jit(solution)/shard_map/psum | solution.py:58
  328.1 0.9 multiply_reduce_fusion.4
  329.1 24.4 %all_gather.15 = bf16[128,128]{1,0:T(8,128)(2,1)S(1)} all-gather(bf16[8,128]{1,0:T(8,128)(2,1)S(1)} %get-tuple-element.12), channel_id=1, replica_groups=mesh['row'=16,'col'=16] {'row'}, dimensions={0}, use_global_device_ids=true | all-gather | bytes 34816 | tf_op jit(solution)/shard_map/all_gather | solution.py:40
  353.5 0.7 multiply_reduce_fusion.6
  354.2 28.8 %all_gather.14 = bf16[256,128]{1,0:T(8,128)(2,1)S(1)} all-gather(bf16[16,128]{1,0:T(8,128)(2,1)S(1)} %get-tuple-element.10), channel_id=1, replica_groups=mesh['row'=16,'col'=16] {'col'}, dimensions={0}, use_global_device_ids=true | all-gather | bytes 69632 | tf_op jit(solution)/shard_map/all_gather | solution.py:39
  383.0 5.6 multiply_convert_fusion
  388.6 8.1 %fusion = bf16[32768,128]{1,0:T(8,128)(2,1)S(1)} fusion(bf16[32768,128]{1,0:T(8,128)(2,1)} %bitcast.19, bf16[128,128]{1,0:T(8,128)(2,1)S(1)} %get-tuple-element.8, bf16[32768,128]{1,0:T(8,128)(2,1)} %bitcast.26), kind=kOutput, calls=%fused_computation.1 | convolution fusion | flops 1086324736 | bytes 25198592 | tf_op jit(solution)/shard_map/dot_general | solution.py:23
  396.8 3.2 copy-done.1
  400.0 6.4 fusion.12
  406.4 12.1 %multiply_reduce_fusion.1 = (bf16[256,128]{1,0:T(8,128)(2,1)}, f32[32768,128]{1,0:T(8,128)}) fusion(f32[128,128]{1,0:T(8,128)S(1)} %convert_element_type.126, bf16[32768,128]{1,0:T(8,128)(2,1)} %copy-done.1, bf16[128,128]{1,0:T(8,128)(2,1)S(1)} %get-tuple-element.8), kind=kOutput, calls=%fused_computation.5 | convolution fusion | flops 1082097664 | bytes 25329664 | tf_op jit(solution)/shard_map/dot_general | solution.py:25
  418.4 0.0 reduce-scatter.5.cloned.1.call-start
  418.5 7.3 %multiply_reduce_fusion = bf16[128,128]{1,0:T(8,128)(2,1)S(1)} fusion(f32[256,128,128]{2,1,0:T(8,128)} %bitcast.24, f32[256,128]{1,0:T(8,128)S(1)} %convert_element_type.125), kind=kLoop, calls=%fused_computation.4 | loop fusion | flops 8372224 | bytes 16941056 | tf_op jit(solution)/shard_map/reduce_sum | solution.py:27
  425.8 47.7 %all-reduce.1 = bf16[128,128]{1,0:T(8,128)(2,1)S(1)} all-reduce(bf16[128,128]{1,0:T(8,128)(2,1)S(1)} %multiply_reduce_fusion), channel_id=5, replica_groups=mesh['row'=16,'col'=16] {'row'}, use_global_device_ids=true, to_apply=%region_18.0.clone | all-reduce | flops 16384 | bytes 65536
  473.5 86.2 %all-reduce.2 = (f32[128]{0:T(128)S(1)}, f32[128]{0:T(128)S(1)}) all-reduce(f32[128]{0:T(128)S(1)} %get-tuple-element.11, f32[128]{0:T(128)S(1)} %get-tuple-element.9), channel_id=1, replica_groups=mesh['row'=16,'col'=16] {'row','col'}, use_global_device_ids=true, to_apply=%region_10.0 | all-reduce | flops 256 | bytes 2048 | tf_op jit(solution)/shard_map/psum | solution.py:41
  559.7 0.6 multiply_add_fusion.4
  560.3 92.8 %all-reduce.9.cloned.1.call-done = f32[128,128]{1,0:T(8,128)} async-done(((f32[128,128]{1,0:T(8,128)}), f32[128,128]{1,0:T(8,128)}) %all-reduce.9.cloned.1.call-update) | async-done | bytes 65552 | tf_op jit(solution)/shard_map/psum | solution.py:58
  653.2 1.5 multiply_add_fusion
  654.6 1.3 multiply_add_fusion.2
  (30 shorter events, 0.3 us)
Async XLA Ops:
  8.0 69.1 %copy-start.2 = (f32[128,128]{1,0:T(8,128)S(1)}, f32[128,128]{1,0:T(8,128)}, u32[]{:S(2)}) copy-start(f32[128,128]{1,0:T(8,128)} %param.7) | copy-start | bytes 196612
  8.0 320.1 %all-reduce.7.cloned.1.call-start = ((), (), s32[]{:S(2)}) async-start(), calls=%async_computation.3 | async-start | bytes 131072 | tf_op jit(solution)/shard_map/psum | solution.py:58
  85.2 3.2 copy-start
  94.9 258.6 %reduce-scatter.3.cloned.1.call-start = ((), (), s32[]{:S(2)}) async-start(), calls=%async_computation.2 | async-start | bytes 69632 | tf_op jit(solution)/shard_map/reduce_scatter | solution.py:50
  107.0 546.1 %all-reduce.9.cloned.1.call-start = ((), (), s32[]{:S(2)}) async-start(), calls=%async_computation.5 | async-start | bytes 131072 | tf_op jit(solution)/shard_map/psum | solution.py:58
  107.1 53.7 %copy-start.7 = (u32[256]{0:T(256)S(1)}, u32[256]{0:T(256)}, u32[]{:S(2)}) copy-start(u32[256]{0:T(256)} %constant.14) | copy-start | bytes 3076
  107.1 221.9 %copy-start.5 = (f32[8,128]{1,0:T(8,128)S(1)}, f32[8,128]{1,0:T(8,128)}, u32[]{:S(2)}) copy-start(f32[8,128]{1,0:T(8,128)} %param.6) | copy-start | bytes 12292
  107.1 246.4 %copy-start.4 = (f32[16,128]{1,0:T(8,128)S(1)}, f32[16,128]{1,0:T(8,128)}, u32[]{:S(2)}) copy-start(f32[16,128]{1,0:T(8,128)} %param.5) | copy-start | bytes 24580
  396.7 3.2 copy-start.1
  418.4 236.2 %reduce-scatter.5.cloned.1.call-start = ((), (), s32[]{:S(2)}) async-start(), calls=%async_computation.4 | async-start | bytes 69632 | tf_op jit(solution)/shard_map/reduce_scatter | solution.py:50
  418.5 234.7 %copy-start.3 = (f32[128,128]{1,0:T(8,128)S(1)}, f32[128,128]{1,0:T(8,128)}, u32[]{:S(2)}) copy-start(f32[128,128]{1,0:T(8,128)} %all-reduce.7.cloned.1.call-done) | copy-start | bytes 196612
  418.5 236.1 %copy-start.6 = (bf16[16,128]{1,0:T(8,128)(2,1)S(1)}, bf16[16,128]{1,0:T(8,128)(2,1)}, u32[]{:S(2)}) copy-start(bf16[16,128]{1,0:T(8,128)(2,1)} %reduce-scatter.3.cloned.1.call-done) | copy-start | bytes 12292
Sparse Core Ops, SparseCore 0:
  95.0 233.1 all-reduce.6
  418.6 234.5 all-reduce.8
Sparse Core Ops, SparseCore 1:
  107.1 58.3 reduce-scatter.2
  560.4 60.9 reduce-scatter.4
where the time goes:
time: 664 us; the launch traced here: 663 us
  blocking collectives  380 us (57%)
  waiting for transfers between devices  175 us (26%)
  matrix products  53.2 us (8%)
  other arithmetic  32.4 us (5%)
  between operations  16.3 us (2%)
  local copies, waits for them, and re-layouts  7.04 us (1%)
    psum x2, waiting for transfers between devices, local(): grad_c = lax.psum(grad_c, ('row', 'col'))  175 us
    psum x2, blocking collectives, local(): lax.psum((column_squares(a_mine16), column_squares(b_mine16)), ('row', 'c...  171 us
    unnamed x2, blocking collectives  94 us
    all_gather x2, blocking collectives, local(): tile_a = lax.all_gather(a_mine16, 'col', axis=0, tiled=True)  60.5 us
    all_gather x2, blocking collectives, local(): tile_b = lax.all_gather(b_mine16, 'row', axis=0, tiled=True)  54.7 us
    dot_general x2, matrix products, local_terms(): jnp.dot(resid, c16, preferred_element_type=jnp.float32)  24.1 us
    dot_general x2, matrix products, local_terms(): model = jnp.dot(pairs, c16.T, preferred_element_type=jnp.float32)  16.2 us
    reduce_sum x2, other arithmetic, local_terms(): grad_b = jnp.sum(along * tile_a.astype(jnp.float32)[:, None, :], axis=0)  14.7 us
  transfers between devices with their start and end apart: 4, of which 2 were waited for; matrix products, arithmetic and copies ran while one was open for 5% of the time, Pallas kernels for 0%

commit v1 on v0

--- a/solution.py
+++ b/solution.py
@@ -37,7 +37,15 @@
         a_mine16 = own_a.astype(jnp.bfloat16)
         b_mine16 = own_b.astype(jnp.bfloat16)
         tile_a = lax.all_gather(a_mine16, "col", axis=0, tiled=True)
-        tile_b = lax.all_gather(b_mine16, "row", axis=0, tiled=True)
+        tile_b = jnp.concatenate(
+            lax.all_to_all(
+                jnp.stack(tuple((b_mine16 for _ in range(lax.psum(1, "row")))), axis=0),
+                "row",
+                split_axis=0,
+                concat_axis=0,
+            ),
+            axis=0,
+        )
         norm_a, norm_b = lax.psum(
             (column_squares(a_mine16), column_squares(b_mine16)), ("row", "col")
         )

time: 664 us -> 785 us (1.18)
  waiting for transfers between devices: 175 us -> 352 us
  blocking collectives: 380 us -> 308 us
  starting transfers between devices: 0.17 us -> 13.7 us
    psum x2, waiting for transfers between devices: 175 us -> 279 us  [local(): grad_c = lax.psum(grad_c, ('row', 'col'))]
    reduce_scatter x2, waiting for transfers between devices: 0.02 us -> 65.4 us  [local(): lax.psum_scatter(grad_a.astype(jnp.bfloat16), 'col', scatter_dimension=0,...]
    all_gather x2 -> x0, blocking collectives: 54.7 us -> none  [local(): tile_b = lax.all_gather(b_mine16, 'row', axis=0, tiled=True)]
    all_gather x2, blocking collectives: 60.5 us -> 45.8 us  [local(): tile_a = lax.all_gather(a_mine16, 'col', axis=0, tiled=True)]
    all_to_all x0 -> x2, starting transfers between devices: none -> 13.5 us  [local(): lax.all_to_all(jnp.stack(tuple((b_mine16 for _ in range(lax.psum(1, 'row'...]
  transfers between devices with their start and end apart: 4 -> 6, of which waited for: 2 -> 4; matrix products, arithmetic and copies ran while one was open for 5% -> 2% of each run, Pallas kernels for 0% -> 0%
where the time goes in v1:
time: 785 us; the launch traced here: 784 us
  waiting for transfers between devices  352 us (45%)
  blocking collectives  308 us (39%)
  matrix products  53.1 us (7%)
  other arithmetic  32.3 us (4%)
  between operations  16.3 us (2%)
  starting transfers between devices  13.7 us (2%)
  local copies, waits for them, and re-layouts  8.94 us (1%)
    psum x2, waiting for transfers between devices, local(): grad_c = lax.psum(grad_c, ('row', 'col'))  279 us
    psum x2, blocking collectives, local(): lax.psum((column_squares(a_mine16), column_squares(b_mine16)), ('row', 'c...  164 us
    unnamed x2, blocking collectives  97.9 us
    reduce_scatter x2, waiting for transfers between devices, local(): lax.psum_scatter(grad_a.astype(jnp.bfloat16), 'col', scatter_dimension=0,...  65.4 us
    all_gather x2, blocking collectives, local(): tile_a = lax.all_gather(a_mine16, 'col', axis=0, tiled=True)  45.8 us
    dot_general x2, matrix products, local_terms(): jnp.dot(resid, c16, preferred_element_type=jnp.float32)  24.1 us
    dot_general x2, matrix products, local_terms(): model = jnp.dot(pairs, c16.T, preferred_element_type=jnp.float32)  16.2 us
  transfers between devices with their start and end apart: 6, of which 4 were waited for; matrix products, arithmetic and copies ran while one was open for 2% of the time, Pallas kernels for 0%

profile of v1, /device:TPU:1, one launch (start us, length us, event | category | flops | bytes accessed | tf_op | source)
XLA Modules:
  0.0 784.1 jit_solution(3703987832898902721)
XLA Ops:
  8.0 0.7 multiply_reduce_fusion.9
  8.7 0.6 stack.4
  9.4 10.0 %all-to-all-start = ((bf16[16,8,128]{2,1,0:T(8,128)(2,1)}), bf16[16,8,128]{2,1,0:T(8,128)(2,1)S(1)}, u32[]{:S(2)}, u32[]{:S(2)}) async-start(bf16[16,8,128]{2,1,0:T(8,128)(2,1)} %stack.4), calls=%async_computation | async-start | bytes 65536 | tf_op jit(solution)/shard_map/all_to_all | solution.py:41
  19.5 0.7 multiply_reduce_fusion.7
  20.2 77.5 %all-reduce.3 = (f32[128]{0:T(128)S(1)}, f32[128]{0:T(128)S(1)}) all-reduce(f32[128]{0:T(128)S(1)} %get-tuple-element.15, f32[128]{0:T(128)S(1)} %get-tuple-element.13), channel_id=1, replica_groups=mesh['row'=16,'col'=16] {'row','col'}, use_global_device_ids=true, to_apply=%region_6.0 | all-reduce | flops 256 | bytes 2048 | tf_op jit(solution)/shard_map/psum | solution.py:49
  97.6 21.1 %all_gather.6 = bf16[256,128]{1,0:T(8,128)(2,1)S(1)} all-gather(bf16[16,128]{1,0:T(8,128)(2,1)S(1)} %get-tuple-element.16), channel_id=1, replica_groups=mesh['row'=16,'col'=16] {'col'}, dimensions={0}, use_global_device_ids=true | all-gather | bytes 69632 | tf_op jit(solution)/shard_map/all_gather | solution.py:39
  118.7 1.3 dynamic-slice
  120.7 5.6 multiply_convert_fusion.1
  126.3 8.1 %fusion.1 = bf16[32768,128]{1,0:T(8,128)(2,1)S(1)} fusion(bf16[32768,128]{1,0:T(8,128)(2,1)} %bitcast.27, bf16[32768,128]{1,0:T(8,128)(2,1)} %bitcast.31, f32[128,128]{1,0:T(8,128)S(1)} %copy-done.2), kind=kOutput, calls=%fused_computation.3 | convolution fusion | flops 1086341120 | bytes 25231360 | tf_op jit(solution)/shard_map/dot_general | solution.py:23
  134.4 3.2 copy-done.1
  137.6 6.4 fusion.11
  144.0 12.1 %multiply_reduce_fusion.3 = (bf16[256,128]{1,0:T(8,128)(2,1)}, f32[32768,128]{1,0:T(8,128)}) fusion(f32[128,128]{1,0:T(8,128)S(1)} %bitcast_convert_fusion.1, bf16[32768,128]{1,0:T(8,128)(2,1)} %copy-done.1, f32[128,128]{1,0:T(8,128)S(1)} %copy-done.2), kind=kOutput, calls=%fused_computation.8 | convolution fusion | flops 1082114048 | bytes 25362432 | tf_op jit(solution)/shard_map/dot_general | solution.py:25
  156.1 7.3 multiply_reduce_fusion.2
  163.4 48.4 %all-reduce = bf16[128,128]{1,0:T(8,128)(2,1)S(1)} all-reduce(bf16[128,128]{1,0:T(8,128)(2,1)S(1)} %multiply_reduce_fusion.2), channel_id=3, replica_groups=mesh['row'=16,'col'=16] {'row'}, use_global_device_ids=true, to_apply=%region_8.0.clone | all-reduce | flops 16384 | bytes 65536
  211.8 183.3 %all-reduce.7.cloned.1.call-done = f32[128,128]{1,0:T(8,128)} async-done(((f32[128,128]{1,0:T(8,128)}), f32[128,128]{1,0:T(8,128)}) %all-reduce.7.cloned.1.call-update) | async-done | bytes 65552 | tf_op jit(solution)/shard_map/psum | solution.py:66
  395.1 0.9 multiply_reduce_fusion.4
  396.7 3.5 all-to-all-start.1
  400.8 6.7 all-to-all-done.1
  407.5 65.4 %reduce-scatter.3.cloned.1.call-done = bf16[16,128]{1,0:T(8,128)(2,1)} async-done(((bf16[256,128]{1,0:T(8,128)(2,1)}), bf16[16,128]{1,0:T(8,128)(2,1)}) %reduce-scatter.3.cloned.1.call-update) | async-done | bytes 4112 | tf_op jit(solution)/shard_map/reduce_scatter | solution.py:58
  472.9 0.7 multiply_reduce_fusion.6
  473.6 24.7 %all_gather.7 = bf16[256,128]{1,0:T(8,128)(2,1)S(1)} all-gather(bf16[16,128]{1,0:T(8,128)(2,1)S(1)} %get-tuple-element.10), channel_id=1, replica_groups=mesh['row'=16,'col'=16] {'col'}, dimensions={0}, use_global_device_ids=true | all-gather | bytes 69632 | tf_op jit(solution)/shard_map/all_gather | solution.py:39
  498.4 5.6 multiply_convert_fusion
  504.0 8.1 %fusion = bf16[32768,128]{1,0:T(8,128)(2,1)S(1)} fusion(bf16[32768,128]{1,0:T(8,128)(2,1)} %bitcast.25, bf16[128,128]{1,0:T(8,128)(2,1)S(1)} %get-tuple-element.8, bf16[32768,128]{1,0:T(8,128)(2,1)} %bitcast.32), kind=kOutput, calls=%fused_computation.1 | convolution fusion | flops 1086324736 | bytes 25198592 | tf_op jit(solution)/shard_map/dot_general | solution.py:23
  512.1 3.2 copy-done
  515.3 6.4 fusion.12
  521.7 12.1 %multiply_reduce_fusion.1 = (bf16[256,128]{1,0:T(8,128)(2,1)}, f32[32768,128]{1,0:T(8,128)}) fusion(f32[128,128]{1,0:T(8,128)S(1)} %bitcast_convert_fusion, bf16[32768,128]{1,0:T(8,128)(2,1)} %copy-done, bf16[128,128]{1,0:T(8,128)(2,1)S(1)} %get-tuple-element.8), kind=kOutput, calls=%fused_computation.5 | convolution fusion | flops 1082097664 | bytes 25329664 | tf_op jit(solution)/shard_map/dot_general | solution.py:25
  533.9 7.3 multiply_reduce_fusion
  541.2 49.5 %all-reduce.1 = bf16[128,128]{1,0:T(8,128)(2,1)S(1)} all-reduce(bf16[128,128]{1,0:T(8,128)(2,1)S(1)} %multiply_reduce_fusion), channel_id=5, replica_groups=mesh['row'=16,'col'=16] {'row'}, use_global_device_ids=true, to_apply=%region_18.0.clone | all-reduce | flops 16384 | bytes 65536
  590.7 86.9 %all-reduce.2 = (f32[128]{0:T(128)S(1)}, f32[128]{0:T(128)S(1)}) all-reduce(f32[128]{0:T(128)S(1)} %get-tuple-element.11, f32[128]{0:T(128)S(1)} %get-tuple-element.9), channel_id=1, replica_groups=mesh['row'=16,'col'=16] {'row','col'}, use_global_device_ids=true, to_apply=%region_10.0 | all-reduce | flops 256 | bytes 2048 | tf_op jit(solution)/shard_map/psum | solution.py:49
  678.2 95.7 %all-reduce.9.cloned.1.call-done = f32[128,128]{1,0:T(8,128)} async-done(((f32[128,128]{1,0:T(8,128)}), f32[128,128]{1,0:T(8,128)}) %all-reduce.9.cloned.1.call-update) | async-done | bytes 65552 | tf_op jit(solution)/shard_map/psum | solution.py:66
  773.9 1.5 multiply_add_fusion
  775.4 1.3 multiply_add_fusion.2
  (32 shorter events, 2.1 us)
Async XLA Ops:
  8.0 118.3 %copy-start.2 = (f32[128,128]{1,0:T(8,128)S(1)}, f32[128,128]{1,0:T(8,128)}, u32[]{:S(2)}) copy-start(f32[128,128]{1,0:T(8,128)} %param.7) | copy-start | bytes 196612
  9.4 111.3 %all-to-all-start = ((bf16[16,8,128]{2,1,0:T(8,128)(2,1)}), bf16[16,8,128]{2,1,0:T(8,128)(2,1)S(1)}, u32[]{:S(2)}, u32[]{:S(2)}) async-start(bf16[16,8,128]{2,1,0:T(8,128)(2,1)} %stack.4), calls=%async_computation | async-start | bytes 65536 | tf_op jit(solution)/shard_map/all_to_all | solution.py:41
  19.4 375.7 %all-reduce.7.cloned.1.call-start = ((), (), s32[]{:S(2)}) async-start(), calls=%async_computation.5 | async-start | bytes 131072 | tf_op jit(solution)/shard_map/psum | solution.py:66
  134.4 3.2 copy-start.1
  156.1 239.9 %copy-start.5 = (f32[8,128]{1,0:T(8,128)S(1)}, f32[8,128]{1,0:T(8,128)}, u32[]{:S(2)}) copy-start(f32[8,128]{1,0:T(8,128)} %param.6) | copy-start | bytes 12292
  156.1 316.8 %copy-start.4 = (f32[16,128]{1,0:T(8,128)S(1)}, f32[16,128]{1,0:T(8,128)}, u32[]{:S(2)}) copy-start(f32[16,128]{1,0:T(8,128)} %param.5) | copy-start | bytes 24580
  396.7 10.8 %all-to-all-start.1 = ((bf16[16,8,128]{2,1,0:T(8,128)(2,1)}), bf16[16,8,128]{2,1,0:T(8,128)(2,1)S(1)}, u32[]{:S(2)}, u32[]{:S(2)}) async-start(bf16[16,8,128]{2,1,0:T(8,128)(2,1)} %stack.5), calls=%async_computation.2 | async-start | bytes 65536 | tf_op jit(solution)/shard_map/all_to_all | solution.py:41
  400.2 72.7 %reduce-scatter.3.cloned.1.call-start = ((), (), s32[]{:S(2)}) async-start(), calls=%async_computation.4 | async-start | bytes 69632 | tf_op jit(solution)/shard_map/reduce_scatter | solution.py:58
  400.7 373.2 %all-reduce.9.cloned.1.call-start = ((), (), s32[]{:S(2)}) async-start(), calls=%async_computation.7 | async-start | bytes 131072 | tf_op jit(solution)/shard_map/psum | solution.py:66
  512.1 3.2 copy-start
  533.8 241.6 %reduce-scatter.5.cloned.1.call-start = ((), (), s32[]{:S(2)}) async-start(), calls=%async_computation.6 | async-start | bytes 69632 | tf_op jit(solution)/shard_map/reduce_scatter | solution.py:58
  533.9 240.0 %copy-start.3 = (f32[128,128]{1,0:T(8,128)S(1)}, f32[128,128]{1,0:T(8,128)}, u32[]{:S(2)}) copy-start(f32[128,128]{1,0:T(8,128)} %all-reduce.7.cloned.1.call-done) | copy-start | bytes 196612
  533.9 241.5 %copy-start.6 = (bf16[16,128]{1,0:T(8,128)(2,1)S(1)}, bf16[16,128]{1,0:T(8,128)(2,1)}, u32[]{:S(2)}) copy-start(bf16[16,128]{1,0:T(8,128)(2,1)} %reduce-scatter.3.cloned.1.call-done) | copy-start | bytes 12292
Sparse Core Ops, SparseCore 0:
  156.2 238.8 all-reduce.6
  533.9 239.9 all-reduce.8
Sparse Core Ops, SparseCore 1:
  405.1 67.8 reduce-scatter.2
  678.3 61.0 reduce-scatter.4
